TPU v7x, 32 devices: a whole 2x2x4 slice. The times are simulated.
32 devices in a mesh: scen: 2 (over x), hour: 4 (over z), reg: 4 (over y, core).
Axes of the slice: x: 2, y: 2, z: 4, core: 2. Of those that a mesh axis runs over, the one named last changes fastest.
Arguments:
- cost_rate: float32 [8, 672, 2048], P('scen', 'hour', 'reg'), may hold values from 0.05 to 1
- invest_cost: float32 [3, 2048], P(None, 'reg'), may hold values from 0.1 to 1
- tile: bfloat16 [4, 256, 2048], P('hour', None, 'reg'), may hold values from -0.1875 to 0.1875
- tile_mask: int32 [4, 256, 2048], P('hour', None, 'reg'), may hold values 0 or 1
- demand: float32 [8, 672, 256], P('scen', 'hour'), may hold values from -6 to 6
- dispatch: float32 [8, 672, 2048], P('scen', 'hour', 'reg'), may hold values from 0 to 1
- dual: float32 [8, 672, 256], P('scen', 'hour'), may hold values from 0 to 1
- cap_dual: float32 [8, 672, 2048], P('scen', 'hour', 'reg'), may hold values from 0 to 1
- capacity: float32 [8, 3, 2048], P('scen', None, 'reg'), may hold values from 0 to 2
- multiplier: float32 [8, 3, 2048], P('scen', None, 'reg'), may hold values from -3 to 3
- consensus: float32 [8, 3, 2048], P('scen', None, 'reg'), may hold values from 0 to 2
- scen_weight: float32 [8], P('scen'), may hold values from 0.1 to 1
- node_of: int32 [3, 8], P(None, 'scen'), may hold values from 0 to 3, as said below
Outputs:
- dispatch_out: float32 [8, 672, 2048], P('scen', 'hour', 'reg')
- dual_out: float32 [8, 672, 256], P('scen', 'hour', 'reg')
- capacity_out: float32 [8, 3, 2048], P('scen', None, 'reg')
- multiplier_out: float32 [8, 3, 2048], P('scen', None, 'reg')
Inputs may be any that keep to these rules, and one draw needn't show every extreme that they name: `node_of`: at each section the nodes are runs of consecutive scenarios, numbered in order from 0; each node of a section lies within one node of the section before; section 0 is one node, the last section has 4 nodes, and node counts grow from section to section.
All inputs are finite; a program needn't handle non-finite values. No bound on the sum of `tile_mask` on one device may be relied on, other than what follows from the above.
Results may differ from a plain program's by a relative error of at most 0.0015.
Values may be sent and summed in bfloat16 or wider, within the bound.
No kernel may reach another device: no remote copies, remote signals or barrier semaphores. Data moves between devices by JAX's collectives and lax.ppermute only.
A program may use at most 64 MiB of HBM per device.

v0:
```python
import jax
import jax.numpy as jnp
from jax import lax
from jax.sharding import PartitionSpec as P

ITERS = 8
RAMP_WEIGHT = 0.5
PENALTY = 1.0
STEP_PRIMAL = 0.3
STEP_INVEST = 0.5
STEP_DUAL = 0.3
STEP_CAP = 0.05


def with_halo(cells, sides, width):
    for axis, dim in sides:
        count = lax.axis_size(axis)
        ends = count - 1
        head = lax.slice_in_dim(cells, 0, width, axis=dim)
        tail = lax.slice_in_dim(cells, cells.shape[dim] - width, cells.shape[dim], axis=dim)
        cells = jnp.concatenate(
            [
                lax.ppermute(tail, axis, [(i, (i + 1) % count) for i in range(ends)]),
                cells,
                lax.ppermute(head, axis, [((i + 1) % count, i) for i in range(ends)]),
            ],
            axis=dim,
        )
    return cells


def safe_average(node_sum, node_mass):
    safe_mass = node_mass + (node_mass <= 0.0).astype(jnp.float32)
    return node_sum / safe_mass[:, :, None]


def shards(
    cost_rate,
    invest_cost,
    tile,
    tile_mask,
    demand,
    dispatch,
    dual,
    cap_dual,
    capacity,
    multiplier,
    consensus,
    scen_weight,
    node_of,
):
    matrix = tile[0] * tile_mask[0].astype(jnp.bfloat16)
    hours_all = dispatch.shape[1] * lax.axis_size("hour")
    reg_count = lax.axis_size("reg")
    reg_place = lax.axis_index("reg")
    cons_part = dual.shape[2] // reg_count
    first_row = reg_place * cons_part
    primal = dispatch
    cap_var = cap_dual
    invest = capacity
    dual_low = dual.astype(jnp.bfloat16)
    dual_var = lax.dynamic_slice_in_dim(dual, first_row, cons_part, 2)
    demand_use = lax.dynamic_slice_in_dim(demand, first_row, cons_part, 2)
    for step_index in range(ITERS):
        padded = with_halo(primal, (("hour", 1),), 1)
        rough = 2.0 * primal - padded[:, :-2] - padded[:, 2:]
        pulled = jnp.einsum("shr,rc->shc", dual_low, matrix, preferred_element_type=jnp.float32)
        grad_x = cost_rate + RAMP_WEIGHT * rough - pulled + cap_var
        zmean = lax.psum(jnp.sum(cap_var, axis=1), "hour") / hours_all
        grad_u = invest_cost[None] + multiplier + PENALTY * (invest - consensus) - zmean[:, None, :]
        primal_new = jnp.maximum(primal - STEP_PRIMAL * grad_x, 0.0)
        invest_new = jnp.maximum(invest - STEP_INVEST * grad_u, 0.0)
        primal_ext = 2.0 * primal_new - primal
        invest_ext = 2.0 * invest_new - invest
        partial_rows = jnp.einsum(
            "shc,rc->shr",
            primal_ext.astype(jnp.bfloat16),
            matrix,
            preferred_element_type=jnp.float32,
        )
        image = lax.psum_scatter(partial_rows, "reg", scatter_dimension=2, tiled=True)
        dual_var = jnp.maximum(dual_var + STEP_DUAL * (demand_use - image), 0.0)
        if step_index + 1 < ITERS:
            dual_low = lax.all_gather(dual_var.astype(jnp.bfloat16), "reg", axis=2, tiled=True)
        cap_var = jnp.maximum(
            cap_var + STEP_CAP * (primal_ext - jnp.sum(invest_ext, axis=1)[:, None, :]), 0.0
        )
        primal = primal_new
        invest = invest_new
    node_count = node_of.shape[1] * lax.axis_size("scen") // 2
    node_ids = jnp.arange(node_count, dtype=jnp.int32)
    one_hot = (node_of[:, :, None] == node_ids[None, None, :]).astype(jnp.float32)
    weighted = scen_weight[:, None, None] * invest
    node_sum = jnp.einsum("gsn,sgc->gnc", one_hot, weighted, precision=lax.Precision.HIGHEST)
    node_mass = jnp.einsum("gsn,s->gn", one_hot, scen_weight, precision=lax.Precision.HIGHEST)
    sum_total, mass_total = lax.psum((node_sum, node_mass), "scen")
    average = safe_average(sum_total, mass_total)
    spread_back = jnp.einsum("gsn,gnc->sgc", one_hot, average, precision=lax.Precision.HIGHEST)
    multiplier_out = multiplier + PENALTY * (invest - spread_back)
    return (primal, dual_var, invest, multiplier_out)


def solution(mesh):
    placed = (
        P("scen", "hour", "reg"),
        P(None, "reg"),
        P("hour", None, "reg"),
        P("hour", None, "reg"),
        P("scen", "hour", None),
        P("scen", "hour", "reg"),
        P("scen", "hour", None),
        P("scen", "hour", "reg"),
        P("scen", None, "reg"),
        P("scen", None, "reg"),
        P("scen", None, "reg"),
        P("scen"),
        P(None, "scen"),
    )
    return jax.shard_map(
        shards,
        mesh=mesh,
        in_specs=placed,
        out_specs=(
            P("scen", "hour", "reg"),
            P("scen", "hour", "reg"),
            P("scen", None, "reg"),
            P("scen", None, "reg"),
        ),
        check_vma=False,
    )
```

profile of v0, /device:TPU:0, one launch (start us, length us, event | category | flops | bytes accessed | tf_op | source)
XLA Modules:
  0.0 344.3 jit_solution(13150075542989649014)
XLA Ops:
  8.3 5.0 %collective-permute-start = (f32[4,1,512]{2,1,0:T(1,128)S(1)}, f32[4,1,512]{2,1,0:T(1,128)S(1)}, u32[]{:S(2)}, u32[]{:S(2)}) collective-permute-start(f32[4,1,512]{2,1,0:T(1,128)S(1)} %get-tuple-element.40), channel_id=1, source_target_pairs={{0,4},{4,8},{8,12},{1,5},{5,9},{9,13},{2,6},{6,10},{10,14},{3,7},{... | collective-permute-start | bytes 24584 | tf_op jit(solution)/shard_map/ppermute | solution.py:23
  16.1 13.2 %psum.70 = f32[4,512]{1,0:T(4,128)S(1)} all-reduce(f32[4,512]{1,0:T(4,128)S(1)} %reduce_sum.135), channel_id=1, replica_groups=mesh['scen'=2,'hour'=4,'reg'=4] {'hour'}, use_global_device_ids=true, to_apply=%region_2.0 | all-reduce | flops 2048 | bytes 16384 | tf_op jit(solution)/shard_map/psum | solution.py:69
  29.4 5.6 %fusion.161 = (f32[4,512]{1,0:T(4,128)S(1)}, f32[4,168,512]{2,1,0:T(8,128)}, f32[4,168,512]{2,1,0:T(8,128)S(1)}) fusion(f32[4,168,512]{2,1,0:T(8,128)} %param.20, f32[4,512]{1,0:T(4,128)S(1)} %get-tuple-element.24, f32[4,168,512]{2,1,0:T(8,128)} %param.18, f32[4,168,256]{2,1,0:T(8,128)S(1)} %copy-done.19, ...), kind=kOutput, calls=%fused_computation.216 | convolution fusion | flops 182867968 | bytes 7864320 | tf_op jit(solution)/shard_map/shr,rc->shc/dot_general | solution.py:67
  41.0 11.5 %psum.71 = f32[4,512]{1,0:T(4,128)S(1)} all-reduce(f32[4,512]{1,0:T(4,128)S(1)} %get-tuple-element.22), channel_id=1, replica_groups=mesh['scen'=2,'hour'=4,'reg'=4] {'hour'}, use_global_device_ids=true, to_apply=%region_6.0 | all-reduce | flops 2048 | bytes 16384 | tf_op jit(solution)/shard_map/psum | solution.py:69
  52.5 7.2 %reduce-scatter.9.cloned.1.call-done = f32[4,168,64]{1,2,0:T(8,128)} async-done(((f32[4,168,256]{1,2,0:T(8,128)}), f32[4,168,64]{1,2,0:T(8,128)}) %reduce-scatter.9.cloned.1.call-update) | async-done | bytes 172048 | tf_op jit(solution)/shard_map/reduce_scatter | solution.py:81
  60.9 6.6 %all_gather.21 = bf16[4,168,256]{1,2,0:T(8,128)(2,1)S(1)} all-gather(bf16[4,168,64]{1,2,0:T(8,128)(2,1)S(1)} %fusion.131), channel_id=1, replica_groups=mesh['scen'=2,'hour'=4,'reg'=4] {'reg'}, dimensions={2}, use_global_device_ids=true | all-gather | bytes 430080 | tf_op jit(solution)/shard_map/all_gather | solution.py:84
  67.5 3.6 %fusion.159 = (f32[4,512]{1,0:T(4,128)S(1)}, f32[4,168,512]{2,1,0:T(8,128)}, f32[4,168,512]{2,1,0:T(8,128)S(1)}) fusion(f32[4,168,512]{2,1,0:T(8,128)} %get-tuple-element.23, f32[4,512]{1,0:T(4,128)S(1)} %subtract_reduce_fusion.5, f32[4,168,512]{2,1,0:T(8,128)S(1)} %get-tuple-element.42, bf16[4,168,256]{1,2,0:T(8,128)(2,1)S(1)} %all_gather.21, ...), kind=kOutput, calls=%fused_computation.214 | convolution fusion | flops 182695936 | bytes 7520256 | tf_op jit(solution)/shard_map/shr,rc->shc/dot_general | solution.py:67
  79.4 13.1 %psum.72 = f32[4,512]{1,0:T(4,128)S(1)} all-reduce(f32[4,512]{1,0:T(4,128)S(1)} %get-tuple-element.18), channel_id=1, replica_groups=mesh['scen'=2,'hour'=4,'reg'=4] {'hour'}, use_global_device_ids=true, to_apply=%region_10.0 | all-reduce | flops 2048 | bytes 16384 | tf_op jit(solution)/shard_map/psum | solution.py:69
  92.6 6.6 %reduce-scatter.11.cloned.1.call-done = f32[4,168,64]{1,2,0:T(8,128)} async-done(((f32[4,168,256]{1,2,0:T(8,128)}), f32[4,168,64]{1,2,0:T(8,128)}) %reduce-scatter.11.cloned.1.call-update) | async-done | bytes 172048 | tf_op jit(solution)/shard_map/reduce_scatter | solution.py:81
  100.2 6.6 %all_gather.22 = bf16[4,168,256]{1,2,0:T(8,128)(2,1)S(1)} all-gather(bf16[4,168,64]{1,2,0:T(8,128)(2,1)S(1)} %get-tuple-element.20), channel_id=1, replica_groups=mesh['scen'=2,'hour'=4,'reg'=4] {'reg'}, dimensions={2}, use_global_device_ids=true | all-gather | bytes 430080 | tf_op jit(solution)/shard_map/all_gather | solution.py:84
  106.8 4.0 %fusion.158 = (f32[4,512]{1,0:T(4,128)S(1)}, f32[4,168,512]{2,1,0:T(8,128)}, f32[4,168,512]{2,1,0:T(8,128)S(1)}) fusion(f32[4,168,512]{2,1,0:T(8,128)} %get-tuple-element.19, f32[4,512]{1,0:T(4,128)S(1)} %subtract_reduce_fusion.4, f32[4,168,512]{2,1,0:T(8,128)S(1)} %copy-done.2, bf16[4,168,256]{1,2,0:T(8,128)(2,1)S(1)} %all_gather.22, ...), kind=kOutput, calls=%fused_computation.213 | convolution fusion | flops 182695936 | bytes 7520256 | tf_op jit(solution)/shard_map/shr,rc->shc/dot_general | solution.py:67
  119.1 13.1 %psum.73 = f32[4,512]{1,0:T(4,128)S(1)} all-reduce(f32[4,512]{1,0:T(4,128)S(1)} %get-tuple-element.16), channel_id=1, replica_groups=mesh['scen'=2,'hour'=4,'reg'=4] {'hour'}, use_global_device_ids=true, to_apply=%region_14.0 | all-reduce | flops 2048 | bytes 16384 | tf_op jit(solution)/shard_map/psum | solution.py:69
  132.2 6.7 %reduce-scatter.13.cloned.1.call-done = f32[4,168,64]{1,2,0:T(8,128)} async-done(((f32[4,168,256]{1,2,0:T(8,128)}), f32[4,168,64]{1,2,0:T(8,128)}) %reduce-scatter.13.cloned.1.call-update) | async-done | bytes 172048 | tf_op jit(solution)/shard_map/reduce_scatter | solution.py:81
  139.9 6.6 %all_gather.23 = bf16[4,168,256]{1,2,0:T(8,128)(2,1)S(1)} all-gather(bf16[4,168,64]{1,2,0:T(8,128)(2,1)S(1)} %fusion.132), channel_id=1, replica_groups=mesh['scen'=2,'hour'=4,'reg'=4] {'reg'}, dimensions={2}, use_global_device_ids=true | all-gather | bytes 430080 | tf_op jit(solution)/shard_map/all_gather | solution.py:84
  146.5 5.4 %fusion.156 = (f32[4,512]{1,0:T(4,128)S(1)}, f32[4,168,512]{2,1,0:T(8,128)}, f32[4,168,512]{2,1,0:T(8,128)S(1)}) fusion(f32[4,168,512]{2,1,0:T(8,128)} %get-tuple-element.17, f32[4,512]{1,0:T(4,128)S(1)} %subtract_reduce_fusion.3, f32[4,168,512]{2,1,0:T(8,128)} %copy-done.3, bf16[4,168,256]{1,2,0:T(8,128)(2,1)S(1)} %all_gather.23, ...), kind=kOutput, calls=%fused_computation.211 | convolution fusion | flops 182695936 | bytes 7520256 | tf_op jit(solution)/shard_map/shr,rc->shc/dot_general | solution.py:67
  158.2 13.6 %psum.74 = f32[4,512]{1,0:T(4,128)S(1)} all-reduce(f32[4,512]{1,0:T(4,128)S(1)} %get-tuple-element.12), channel_id=1, replica_groups=mesh['scen'=2,'hour'=4,'reg'=4] {'hour'}, use_global_device_ids=true, to_apply=%region_18.0 | all-reduce | flops 2048 | bytes 16384 | tf_op jit(solution)/shard_map/psum | solution.py:69
  171.9 7.0 %reduce-scatter.15.cloned.1.call-done = f32[4,168,64]{1,2,0:T(8,128)} async-done(((f32[4,168,256]{1,2,0:T(8,128)}), f32[4,168,64]{1,2,0:T(8,128)}) %reduce-scatter.15.cloned.1.call-update) | async-done | bytes 172048 | tf_op jit(solution)/shard_map/reduce_scatter | solution.py:81
  180.1 6.8 %all_gather.24 = bf16[4,168,256]{1,2,0:T(8,128)(2,1)S(1)} all-gather(bf16[4,168,64]{1,2,0:T(8,128)(2,1)S(1)} %get-tuple-element.14), channel_id=1, replica_groups=mesh['scen'=2,'hour'=4,'reg'=4] {'reg'}, dimensions={2}, use_global_device_ids=true | all-gather | bytes 430080 | tf_op jit(solution)/shard_map/all_gather | solution.py:84
  186.9 3.6 %fusion.155 = (f32[4,512]{1,0:T(4,128)S(1)}, f32[4,168,512]{2,1,0:T(8,128)}, f32[4,168,512]{2,1,0:T(8,128)S(1)}) fusion(f32[4,168,512]{2,1,0:T(8,128)} %get-tuple-element.13, f32[4,512]{1,0:T(4,128)S(1)} %subtract_reduce_fusion.2, f32[4,168,512]{2,1,0:T(8,128)S(1)} %get-tuple-element.45, bf16[4,168,256]{1,2,0:T(8,128)(2,1)S(1)} %all_gather.24, ...), kind=kOutput, calls=%fused_computation.210 | convolution fusion | flops 182695936 | bytes 7520256 | tf_op jit(solution)/shard_map/shr,rc->shc/dot_general | solution.py:67
  198.7 13.1 %psum.75 = f32[4,512]{1,0:T(4,128)S(1)} all-reduce(f32[4,512]{1,0:T(4,128)S(1)} %get-tuple-element.10), channel_id=1, replica_groups=mesh['scen'=2,'hour'=4,'reg'=4] {'hour'}, use_global_device_ids=true, to_apply=%region_22.0 | all-reduce | flops 2048 | bytes 16384 | tf_op jit(solution)/shard_map/psum | solution.py:69
  211.9 6.7 %reduce-scatter.17.cloned.1.call-done = f32[4,168,64]{1,2,0:T(8,128)} async-done(((f32[4,168,256]{1,2,0:T(8,128)}), f32[4,168,64]{1,2,0:T(8,128)}) %reduce-scatter.17.cloned.1.call-update) | async-done | bytes 172048 | tf_op jit(solution)/shard_map/reduce_scatter | solution.py:81
  219.6 6.6 %all_gather.25 = bf16[4,168,256]{1,2,0:T(8,128)(2,1)S(1)} all-gather(bf16[4,168,64]{1,2,0:T(8,128)(2,1)S(1)} %fusion.133), channel_id=1, replica_groups=mesh['scen'=2,'hour'=4,'reg'=4] {'reg'}, dimensions={2}, use_global_device_ids=true | all-gather | bytes 430080 | tf_op jit(solution)/shard_map/all_gather | solution.py:84
  226.2 5.4 %fusion.153 = (f32[4,512]{1,0:T(4,128)S(1)}, f32[4,168,512]{2,1,0:T(8,128)}, f32[4,168,512]{2,1,0:T(8,128)S(1)}) fusion(f32[4,168,512]{2,1,0:T(8,128)} %get-tuple-element.11, f32[4,512]{1,0:T(4,128)S(1)} %subtract_reduce_fusion.1, f32[4,168,512]{2,1,0:T(8,128)} %copy-done.5, bf16[4,168,256]{1,2,0:T(8,128)(2,1)S(1)} %all_gather.25, ...), kind=kOutput, calls=%fused_computation.208 | convolution fusion | flops 182695936 | bytes 7520256 | tf_op jit(solution)/shard_map/shr,rc->shc/dot_general | solution.py:67
  233.2 4.0 %collective-permute-start.12 = (f32[4,1,512]{2,1,0:T(1,128)S(1)}, f32[4,1,512]{2,1,0:T(1,128)}, u32[]{:S(2)}, u32[]{:S(2)}) collective-permute-start(f32[4,1,512]{2,1,0:T(1,128)S(1)} %get-tuple-element.28), channel_id=1, source_target_pairs={{0,4},{4,8},{8,12},{1,5},{5,9},{9,13},{2,6},{6,10},{10,14},{3,7},{... | collective-permute-start | bytes 24584 | tf_op jit(solution)/shard_map/ppermute | solution.py:23
  238.4 13.0 %psum.76 = f32[4,512]{1,0:T(4,128)S(1)} all-reduce(f32[4,512]{1,0:T(4,128)S(1)} %get-tuple-element.6), channel_id=1, replica_groups=mesh['scen'=2,'hour'=4,'reg'=4] {'hour'}, use_global_device_ids=true, to_apply=%region_26.0 | all-reduce | flops 2048 | bytes 16384 | tf_op jit(solution)/shard_map/psum | solution.py:69
  251.6 7.0 %reduce-scatter.19.cloned.1.call-done = f32[4,168,64]{1,2,0:T(8,128)} async-done(((f32[4,168,256]{1,2,0:T(8,128)}), f32[4,168,64]{1,2,0:T(8,128)}) %reduce-scatter.19.cloned.1.call-update) | async-done | bytes 172048 | tf_op jit(solution)/shard_map/reduce_scatter | solution.py:81
  259.7 6.6 %all_gather.26 = bf16[4,168,256]{1,2,0:T(8,128)(2,1)S(1)} all-gather(bf16[4,168,64]{1,2,0:T(8,128)(2,1)S(1)} %get-tuple-element.8), channel_id=1, replica_groups=mesh['scen'=2,'hour'=4,'reg'=4] {'reg'}, dimensions={2}, use_global_device_ids=true | all-gather | bytes 430080 | tf_op jit(solution)/shard_map/all_gather | solution.py:84
  277.1 19.9 %reduce-scatter.21.cloned.1.call-done = f32[4,168,64]{1,2,0:T(8,128)} async-done(((f32[4,168,256]{1,2,0:T(8,128)}), f32[4,168,64]{1,2,0:T(8,128)}) %reduce-scatter.21.cloned.1.call-update) | async-done | bytes 172048 | tf_op jit(solution)/shard_map/reduce_scatter | solution.py:81
  298.1 6.6 %all_gather.27 = bf16[4,168,256]{1,2,0:T(8,128)(2,1)S(1)} all-gather(bf16[4,168,64]{1,2,0:T(8,128)(2,1)S(1)} %fusion.134), channel_id=1, replica_groups=mesh['scen'=2,'hour'=4,'reg'=4] {'reg'}, dimensions={2}, use_global_device_ids=true | all-gather | bytes 430080 | tf_op jit(solution)/shard_map/all_gather | solution.py:84
  310.4 11.8 %psum.77 = f32[4,512]{1,0:T(4,128)S(1)} all-reduce(f32[4,512]{1,0:T(4,128)S(1)} %get-tuple-element.48), channel_id=1, replica_groups=mesh['scen'=2,'hour'=4,'reg'=4] {'hour'}, use_global_device_ids=true, to_apply=%region_30.0 | all-reduce | flops 2048 | bytes 16384 | tf_op jit(solution)/shard_map/psum | solution.py:69
  322.7 8.3 %all-reduce = (f32[3,4,512]{2,1,0:T(4,128)S(1)}, f32[3,4]{1,0:T(4,128)S(1)}) all-reduce(f32[3,4,512]{2,1,0:T(4,128)S(1)} %fusion.135, f32[3,4]{1,0:T(4,128)S(1)} %bitcast.85), channel_id=1, replica_groups=mesh['scen'=2,'hour'=4,'reg'=4] {'scen'}, use_global_device_ids=true, to_apply=%region_31.0 | all-reduce | flops 6156 | bytes 49248 | tf_op jit(solution)/shard_map/psum | solution.py:96
  331.8 3.9 %reduce-scatter.23.cloned.1.call-done = f32[4,168,64]{1,2,0:T(8,128)} async-done(((f32[4,168,256]{1,2,0:T(8,128)}), f32[4,168,64]{1,2,0:T(8,128)}) %reduce-scatter.23.cloned.1.call-update) | async-done | bytes 172048 | tf_op jit(solution)/shard_map/reduce_scatter | solution.py:81
  (155 shorter events, 71.0 us)
Async XLA Ops:
  7.2 29.5 %copy-start = (f32[4,168,256]{2,1,0:T(8,128)S(1)}, f32[4,168,256]{2,1,0:T(8,128)}, u32[]{:S(2)}) copy-start(f32[4,168,256]{2,1,0:T(8,128)} %param.17) | copy-start | bytes 2064388
  7.2 22.1 %copy-start.22 = (f32[3,512]{1,0:T(4,128)S(1)}, f32[3,512]{1,0:T(4,128)}, u32[]{:S(2)}) copy-start(f32[3,512]{1,0:T(4,128)} %param.14) | copy-start | bytes 18436
  7.2 22.2 %copy-start.19 = (f32[4,168,256]{2,1,0:T(8,128)S(1)}, f32[4,168,256]{2,1,0:T(8,128)}, u32[]{:S(2)}) copy-start(f32[4,168,256]{2,1,0:T(8,128)} %param.19) | copy-start | bytes 2064388
  7.3 52.5 %reduce-scatter.9.cloned.1.call-start = ((), (), s32[]{:S(2)}) async-start(), calls=%async_computation.8 | async-start | bytes 1310720 | tf_op jit(solution)/shard_map/reduce_scatter | solution.py:81
  8.3 21.1 %collective-permute-start = (f32[4,1,512]{2,1,0:T(1,128)S(1)}, f32[4,1,512]{2,1,0:T(1,128)S(1)}, u32[]{:S(2)}, u32[]{:S(2)}) collective-permute-start(f32[4,1,512]{2,1,0:T(1,128)S(1)} %get-tuple-element.40), channel_id=1, source_target_pairs={{0,4},{4,8},{8,12},{1,5},{5,9},{9,13},{2,6},{6,10},{10,14},{3,7},{... | collective-permute-start | bytes 24584 | tf_op jit(solution)/shard_map/ppermute | solution.py:23
  13.3 16.1 %collective-permute-start.1 = (f32[4,1,512]{2,1,0:T(1,128)S(1)}, f32[4,1,512]{2,1,0:T(1,128)S(1)}, u32[]{:S(2)}, u32[]{:S(2)}) collective-permute-start(f32[4,1,512]{2,1,0:T(1,128)S(1)} %get-tuple-element.41), channel_id=1, source_target_pairs={{4,0},{8,4},{12,8},{5,1},{9,5},{13,9},{6,2},{10,6},{14,10},{7,3},{... | collective-permute-start | bytes 24584 | tf_op jit(solution)/shard_map/ppermute | solution.py:25
  36.6 62.6 %reduce-scatter.11.cloned.1.call-start = ((), (), s32[]{:S(2)}) async-start(), calls=%async_computation.9 | async-start | bytes 1310720 | tf_op jit(solution)/shard_map/reduce_scatter | solution.py:81
  38.4 29.1 %collective-permute-start.2 = (f32[4,1,512]{2,1,0:T(1,128)S(1)}, f32[4,1,512]{2,1,0:T(1,128)S(1)}, u32[]{:S(2)}, u32[]{:S(2)}) collective-permute-start(f32[4,1,512]{2,1,0:T(1,128)S(1)} %get-tuple-element.38), channel_id=1, source_target_pairs={{0,4},{4,8},{8,12},{1,5},{5,9},{9,13},{2,6},{6,10},{10,14},{3,7},{... | collective-permute-start | bytes 24584 | tf_op jit(solution)/shard_map/ppermute | solution.py:23
  39.7 27.8 %collective-permute-start.3 = (f32[4,1,512]{2,1,0:T(1,128)S(1)}, f32[4,1,512]{2,1,0:T(1,128)S(1)}, u32[]{:S(2)}, u32[]{:S(2)}) collective-permute-start(f32[4,1,512]{2,1,0:T(1,128)S(1)} %get-tuple-element.39), channel_id=1, source_target_pairs={{4,0},{8,4},{12,8},{5,1},{9,5},{13,9},{6,2},{10,6},{14,10},{7,3},{... | collective-permute-start | bytes 24584 | tf_op jit(solution)/shard_map/ppermute | solution.py:25
  73.7 25.5 %copy-start.14 = (f32[4,168,64]{1,2,0:T(8,128)S(1)}, f32[4,168,64]{1,2,0:T(8,128)}, u32[]{:S(2)}) copy-start(f32[4,168,64]{1,2,0:T(8,128)} %reduce-scatter.9.cloned.1.call-done) | copy-start | bytes 516100
  73.7 33.2 %copy-start.2 = (f32[4,168,512]{2,1,0:T(8,128)S(1)}, f32[4,168,512]{2,1,0:T(8,128)}, u32[]{:S(2)}) copy-start(f32[4,168,512]{2,1,0:T(8,128)} %copy-done.1) | copy-start | bytes 4128772
  73.7 65.2 %reduce-scatter.13.cloned.1.call-start = ((), (), s32[]{:S(2)}) async-start(), calls=%async_computation.10 | async-start | bytes 1310720 | tf_op jit(solution)/shard_map/reduce_scatter | solution.py:81
  74.7 32.1 %collective-permute-start.4 = (f32[4,1,512]{2,1,0:T(1,128)S(1)}, f32[4,1,512]{2,1,0:T(1,128)S(1)}, u32[]{:S(2)}, u32[]{:S(2)}) collective-permute-start(f32[4,1,512]{2,1,0:T(1,128)S(1)} %get-tuple-element.36), channel_id=1, source_target_pairs={{0,4},{4,8},{8,12},{1,5},{5,9},{9,13},{2,6},{6,10},{10,14},{3,7},{... | collective-permute-start | bytes 24584 | tf_op jit(solution)/shard_map/ppermute | solution.py:23
  78.1 28.7 %collective-permute-start.5 = (f32[4,1,512]{2,1,0:T(1,128)S(1)}, f32[4,1,512]{2,1,0:T(1,128)S(1)}, u32[]{:S(2)}, u32[]{:S(2)}) collective-permute-start(f32[4,1,512]{2,1,0:T(1,128)S(1)} %get-tuple-element.37), channel_id=1, source_target_pairs={{4,0},{8,4},{12,8},{5,1},{9,5},{13,9},{6,2},{10,6},{14,10},{7,3},{... | collective-permute-start | bytes 24584 | tf_op jit(solution)/shard_map/ppermute | solution.py:25
  113.4 65.5 %reduce-scatter.15.cloned.1.call-start = ((), (), s32[]{:S(2)}) async-start(), calls=%async_computation.11 | async-start | bytes 1310720 | tf_op jit(solution)/shard_map/reduce_scatter | solution.py:81
  114.4 32.2 %collective-permute-start.6 = (f32[4,1,512]{2,1,0:T(1,128)S(1)}, f32[4,1,512]{2,1,0:T(1,128)S(1)}, u32[]{:S(2)}, u32[]{:S(2)}) collective-permute-start(f32[4,1,512]{2,1,0:T(1,128)S(1)} %get-tuple-element.34), channel_id=1, source_target_pairs={{0,4},{4,8},{8,12},{1,5},{5,9},{9,13},{2,6},{6,10},{10,14},{3,7},{... | collective-permute-start | bytes 24584 | tf_op jit(solution)/shard_map/ppermute | solution.py:23
  117.8 28.8 %collective-permute-start.7 = (f32[4,1,512]{2,1,0:T(1,128)S(1)}, f32[4,1,512]{2,1,0:T(1,128)S(1)}, u32[]{:S(2)}, u32[]{:S(2)}) collective-permute-start(f32[4,1,512]{2,1,0:T(1,128)S(1)} %get-tuple-element.35), channel_id=1, source_target_pairs={{4,0},{8,4},{12,8},{5,1},{9,5},{13,9},{6,2},{10,6},{14,10},{7,3},{... | collective-permute-start | bytes 24584 | tf_op jit(solution)/shard_map/ppermute | solution.py:25
  153.4 25.5 %copy-start.15 = (f32[4,168,64]{1,2,0:T(8,128)S(1)}, f32[4,168,64]{1,2,0:T(8,128)}, u32[]{:S(2)}) copy-start(f32[4,168,64]{1,2,0:T(8,128)} %reduce-scatter.13.cloned.1.call-done) | copy-start | bytes 516100
  153.4 65.1 %reduce-scatter.17.cloned.1.call-start = ((), (), s32[]{:S(2)}) async-start(), calls=%async_computation.12 | async-start | bytes 1310720 | tf_op jit(solution)/shard_map/reduce_scatter | solution.py:81
  153.5 33.4 %collective-permute-start.8 = (f32[4,1,512]{2,1,0:T(1,128)S(1)}, f32[4,1,512]{2,1,0:T(1,128)S(1)}, u32[]{:S(2)}, u32[]{:S(2)}) collective-permute-start(f32[4,1,512]{2,1,0:T(1,128)S(1)} %get-tuple-element.32), channel_id=1, source_target_pairs={{0,4},{4,8},{8,12},{1,5},{5,9},{9,13},{2,6},{6,10},{10,14},{3,7},{... | collective-permute-start | bytes 24584 | tf_op jit(solution)/shard_map/ppermute | solution.py:23
  156.9 30.0 %collective-permute-start.9 = (f32[4,1,512]{2,1,0:T(1,128)S(1)}, f32[4,1,512]{2,1,0:T(1,128)}, u32[]{:S(2)}, u32[]{:S(2)}) collective-permute-start(f32[4,1,512]{2,1,0:T(1,128)S(1)} %get-tuple-element.33), channel_id=1, source_target_pairs={{4,0},{8,4},{12,8},{5,1},{9,5},{13,9},{6,2},{10,6},{14,10},{7,3},{... | collective-permute-start | bytes 24584 | tf_op jit(solution)/shard_map/ppermute | solution.py:25
  193.1 65.5 %reduce-scatter.19.cloned.1.call-start = ((), (), s32[]{:S(2)}) async-start(), calls=%async_computation.13 | async-start | bytes 1310720 | tf_op jit(solution)/shard_map/reduce_scatter | solution.py:81
  194.0 32.2 %collective-permute-start.10 = (f32[4,1,512]{2,1,0:T(1,128)S(1)}, f32[4,1,512]{2,1,0:T(1,128)S(1)}, u32[]{:S(2)}, u32[]{:S(2)}) collective-permute-start(f32[4,1,512]{2,1,0:T(1,128)S(1)} %get-tuple-element.30), channel_id=1, source_target_pairs={{0,4},{4,8},{8,12},{1,5},{5,9},{9,13},{2,6},{6,10},{10,14},{3,7},{... | collective-permute-start | bytes 24584 | tf_op jit(solution)/shard_map/ppermute | solution.py:23
  197.4 28.8 %collective-permute-start.11 = (f32[4,1,512]{2,1,0:T(1,128)S(1)}, f32[4,1,512]{2,1,0:T(1,128)S(1)}, u32[]{:S(2)}, u32[]{:S(2)}) collective-permute-start(f32[4,1,512]{2,1,0:T(1,128)S(1)} %get-tuple-element.31), channel_id=1, source_target_pairs={{4,0},{8,4},{12,8},{5,1},{9,5},{13,9},{6,2},{10,6},{14,10},{7,3},{... | collective-permute-start | bytes 24584 | tf_op jit(solution)/shard_map/ppermute | solution.py:25
  233.1 25.5 %copy-start.16 = (f32[4,168,64]{1,2,0:T(8,128)S(1)}, f32[4,168,64]{1,2,0:T(8,128)}, u32[]{:S(2)}) copy-start(f32[4,168,64]{1,2,0:T(8,128)} %reduce-scatter.17.cloned.1.call-done) | copy-start | bytes 516100
  233.1 63.9 %reduce-scatter.21.cloned.1.call-start = ((), (), s32[]{:S(2)}) async-start(), calls=%async_computation.14 | async-start | bytes 1310720 | tf_op jit(solution)/shard_map/reduce_scatter | solution.py:81
  233.2 33.2 %collective-permute-start.12 = (f32[4,1,512]{2,1,0:T(1,128)S(1)}, f32[4,1,512]{2,1,0:T(1,128)}, u32[]{:S(2)}, u32[]{:S(2)}) collective-permute-start(f32[4,1,512]{2,1,0:T(1,128)S(1)} %get-tuple-element.28), channel_id=1, source_target_pairs={{0,4},{4,8},{8,12},{1,5},{5,9},{9,13},{2,6},{6,10},{10,14},{3,7},{... | collective-permute-start | bytes 24584 | tf_op jit(solution)/shard_map/ppermute | solution.py:23
  237.1 29.2 %collective-permute-start.13 = (f32[4,1,512]{2,1,0:T(1,128)S(1)}, f32[4,1,512]{2,1,0:T(1,128)}, u32[]{:S(2)}, u32[]{:S(2)}) collective-permute-start(f32[4,1,512]{2,1,0:T(1,128)S(1)} %get-tuple-element.29), channel_id=1, source_target_pairs={{4,0},{8,4},{12,8},{5,1},{9,5},{13,9},{6,2},{10,6},{14,10},{7,3},{... | collective-permute-start | bytes 24584 | tf_op jit(solution)/shard_map/ppermute | solution.py:25
  271.5 64.2 %reduce-scatter.23.cloned.1.call-start = ((), (), s32[]{:S(2)}) async-start(), calls=%async_computation.15 | async-start | bytes 1310720 | tf_op jit(solution)/shard_map/reduce_scatter | solution.py:81
  272.5 32.3 %collective-permute-start.14 = (f32[4,1,512]{2,1,0:T(1,128)S(1)}, f32[4,1,512]{2,1,0:T(1,128)S(1)}, u32[]{:S(2)}, u32[]{:S(2)}) collective-permute-start(f32[4,1,512]{2,1,0:T(1,128)S(1)} %get-tuple-element.26), channel_id=1, source_target_pairs={{0,4},{4,8},{8,12},{1,5},{5,9},{9,13},{2,6},{6,10},{10,14},{3,7},{... | collective-permute-start | bytes 24584 | tf_op jit(solution)/shard_map/ppermute | solution.py:23
  275.8 28.9 %collective-permute-start.15 = (f32[4,1,512]{2,1,0:T(1,128)S(1)}, f32[4,1,512]{2,1,0:T(1,128)S(1)}, u32[]{:S(2)}, u32[]{:S(2)}) collective-permute-start(f32[4,1,512]{2,1,0:T(1,128)S(1)} %get-tuple-element.27), channel_id=1, source_target_pairs={{4,0},{8,4},{12,8},{5,1},{9,5},{13,9},{6,2},{10,6},{14,10},{7,3},{... | collective-permute-start | bytes 24584 | tf_op jit(solution)/shard_map/ppermute | solution.py:25
  310.1 25.6 %copy-start.13 = (f32[4,168,64]{1,2,0:T(8,128)S(1)}, f32[4,168,64]{1,2,0:T(8,128)}, u32[]{:S(2)}) copy-start(f32[4,168,64]{1,2,0:T(8,128)} %reduce-scatter.21.cloned.1.call-done) | copy-start | bytes 516100
  (20 other events, 181.6 us)
Sparse Core Ops, SparseCore 0:
  36.7 23.0 reduce-scatter.8
  73.8 25.3 reduce-scatter.10
  113.6 25.3 reduce-scatter.12
  153.6 25.3 reduce-scatter.14
  193.2 25.3 reduce-scatter.16
  233.2 25.3 reduce-scatter.18
  271.6 25.3 reduce-scatter.20
  310.3 25.3 reduce-scatter.22
where the time goes:
time: 346 us; the launch traced here: 344 us
  blocking collectives  157 us (45%)
  waiting for transfers between devices  65.1 us (19%)
  matrix products  46.1 us (13%)
  starting transfers between devices  37.8 us (11%)
  between operations  14.8 us (4%)
  local copies, waits for them, and re-layouts  11.9 us (3%)
  other arithmetic  11.5 us (3%)
    psum x8, blocking collectives, shards(): zmean = lax.psum(jnp.sum(cap_var, axis=1), 'hour') / hours_all  102 us
    reduce_scatter x8, waiting for transfers between devices, shards(): lax.psum_scatter(partial_rows, 'reg', scatter_dimension=2, tiled=True)  64.9 us
    all_gather x7, blocking collectives, shards(): lax.all_gather(dual_var.astype(jnp.bfloat16), 'reg', axis=2, tiled=True)  46.4 us
    dot_general x8, matrix products, shards(): jnp.einsum('shr,rc->shc', dual_low, matrix, preferred_element_type=jnp.fl...  32.9 us
    ppermute x8, starting transfers between devices, with_halo(): lax.ppermute(tail, axis, [(i, (i + 1) % count) for i in range(ends)])  27.1 us
    dot_general x8, matrix products, shards(): jnp.einsum('shc,rc->shr', primal_ext.astype(jnp.bfloat16), matrix, prefer...  11.9 us
    ppermute x8, starting transfers between devices, with_halo(): lax.ppermute(head, axis, [((i + 1) % count, i) for i in range(ends)])  10.3 us
    psum x1, blocking collectives, shards(): sum_total, mass_total = lax.psum((node_sum, node_mass), 'scen')  8.32 us
  transfers between devices with their start and end apart: 24, of which 8 were waited for; matrix products, arithmetic and copies ran while one was open for 5% of the time, Pallas kernels for 0%

commit v1 on v0

--- a/solution.py
+++ b/solution.py
@@ -66,7 +66,7 @@
         rough = 2.0 * primal - padded[:, :-2] - padded[:, 2:]
         pulled = jnp.einsum("shr,rc->shc", dual_low, matrix, preferred_element_type=jnp.float32)
         grad_x = cost_rate + RAMP_WEIGHT * rough - pulled + cap_var
-        zmean = lax.psum(jnp.sum(cap_var, axis=1), "hour") / hours_all
+        zmean = jnp.sum(lax.all_gather(jnp.sum(cap_var, axis=1), "hour"), axis=0) / hours_all
         grad_u = invest_cost[None] + multiplier + PENALTY * (invest - consensus) - zmean[:, None, :]
         primal_new = jnp.maximum(primal - STEP_PRIMAL * grad_x, 0.0)
         invest_new = jnp.maximum(invest - STEP_INVEST * grad_u, 0.0)

time: 346 us -> 350 us (1.012)
  blocking collectives: 157 us -> 161 us
    all_gather x0 -> x8, blocking collectives: none -> 107 us  [shards(): lax.all_gather(jnp.sum(cap_var, axis=1), 'hour')]
    psum x8 -> x0, blocking collectives: 102 us -> none  [shards(): zmean = lax.psum(jnp.sum(cap_var, axis=1), 'hour') / hours_all]
where the time goes in v1:
time: 350 us; the launch traced here: 348 us
  blocking collectives  161 us (46%)
  waiting for transfers between devices  62.5 us (18%)
  matrix products  46.1 us (13%)
  starting transfers between devices  40.1 us (11%)
  between operations  14.7 us (4%)
  local copies, waits for them, and re-layouts  11.8 us (3%)
  other arithmetic  11.6 us (3%)
    all_gather x8, blocking collectives, shards(): lax.all_gather(jnp.sum(cap_var, axis=1), 'hour')  107 us
    reduce_scatter x8, waiting for transfers between devices, shards(): lax.psum_scatter(partial_rows, 'reg', scatter_dimension=2, tiled=True)  62.4 us
    all_gather x7, blocking collectives, shards(): lax.all_gather(dual_var.astype(jnp.bfloat16), 'reg', axis=2, tiled=True)  46.4 us
    dot_general x8, matrix products, shards(): jnp.einsum('shr,rc->shc', dual_low, matrix, preferred_element_type=jnp.fl...  32.9 us
    ppermute x8, starting transfers between devices, with_halo(): lax.ppermute(tail, axis, [(i, (i + 1) % count) for i in range(ends)])  29.4 us
    dot_general x8, matrix products, shards(): jnp.einsum('shc,rc->shr', primal_ext.astype(jnp.bfloat16), matrix, prefer...  11.9 us
    ppermute x8, starting transfers between devices, with_halo(): lax.ppermute(head, axis, [((i + 1) % count, i) for i in range(ends)])  10.3 us
    psum x1, blocking collectives, shards(): sum_total, mass_total = lax.psum((node_sum, node_mass), 'scen')  8.3 us
  transfers between devices with their start and end apart: 24, of which 8 were waited for; matrix products, arithmetic and copies ran while one was open for 5% of the time, Pallas kernels for 0%

profile of v1, /device:TPU:0, one launch (start us, length us, event | category | flops | bytes accessed | tf_op | source)
XLA Modules:
  0.0 348.3 jit_solution(10665701522728707048)
XLA Ops:
  8.3 5.0 %collective-permute-start = (f32[4,1,512]{2,1,0:T(1,128)S(1)}, f32[4,1,512]{2,1,0:T(1,128)S(1)}, u32[]{:S(2)}, u32[]{:S(2)}) collective-permute-start(f32[4,1,512]{2,1,0:T(1,128)S(1)} %get-tuple-element.40), channel_id=1, source_target_pairs={{0,4},{4,8},{8,12},{1,5},{5,9},{9,13},{2,6},{6,10},{10,14},{3,7},{... | collective-permute-start | bytes 24584 | tf_op jit(solution)/shard_map/ppermute | solution.py:23
  16.1 14.4 %all-gather.8 = f32[4,4,512]{2,1,0:T(4,128)S(1)} all-gather(f32[1,4,512]{2,1,0:T(4,128)S(1)} %bitcast.93), channel_id=2, replica_groups=mesh['scen'=2,'hour'=4,'reg'=4] {'hour'}, dimensions={0}, use_global_device_ids=true | all-gather | bytes 40960 | tf_op jit(solution)/shard_map/all_gather | solution.py:69
  30.7 5.6 %fusion.161 = (f32[4,512]{1,0:T(4,128)S(1)}, f32[4,168,512]{2,1,0:T(8,128)}, f32[4,168,512]{2,1,0:T(8,128)S(1)}) fusion(f32[4,168,512]{2,1,0:T(8,128)} %param.20, f32[4,512]{1,0:T(4,128)S(1)} %get-tuple-element.24, f32[4,168,512]{2,1,0:T(8,128)} %param.18, f32[4,168,256]{2,1,0:T(8,128)S(1)} %copy-done.19, ...), kind=kOutput, calls=%fused_computation.216 | convolution fusion | flops 182867968 | bytes 7864320 | tf_op jit(solution)/shard_map/shr,rc->shc/dot_general | solution.py:67
  39.6 13.1 %all-gather.9 = f32[4,4,512]{2,1,0:T(4,128)S(1)} all-gather(f32[1,4,512]{2,1,0:T(4,128)S(1)} %bitcast.95), channel_id=3, replica_groups=mesh['scen'=2,'hour'=4,'reg'=4] {'hour'}, dimensions={0}, use_global_device_ids=true | all-gather | bytes 40960 | tf_op jit(solution)/shard_map/all_gather | solution.py:69
  52.8 3.5 %collective-permute-start.2 = (f32[4,1,512]{2,1,0:T(1,128)S(1)}, f32[4,1,512]{2,1,0:T(1,128)S(1)}, u32[]{:S(2)}, u32[]{:S(2)}) collective-permute-start(f32[4,1,512]{2,1,0:T(1,128)S(1)} %get-tuple-element.38), channel_id=1, source_target_pairs={{0,4},{4,8},{8,12},{1,5},{5,9},{9,13},{2,6},{6,10},{10,14},{3,7},{... | collective-permute-start | bytes 24584 | tf_op jit(solution)/shard_map/ppermute | solution.py:23
  57.6 6.2 %reduce-scatter.9.cloned.1.call-done = f32[4,168,64]{1,2,0:T(8,128)} async-done(((f32[4,168,256]{1,2,0:T(8,128)}), f32[4,168,64]{1,2,0:T(8,128)}) %reduce-scatter.9.cloned.1.call-update) | async-done | bytes 172048 | tf_op jit(solution)/shard_map/reduce_scatter | solution.py:81
  65.0 6.6 %all_gather.69 = bf16[4,168,256]{1,2,0:T(8,128)(2,1)S(1)} all-gather(bf16[4,168,64]{1,2,0:T(8,128)(2,1)S(1)} %fusion.131), channel_id=1, replica_groups=mesh['scen'=2,'hour'=4,'reg'=4] {'reg'}, dimensions={2}, use_global_device_ids=true | all-gather | bytes 430080 | tf_op jit(solution)/shard_map/all_gather | solution.py:84
  71.6 3.6 %fusion.159 = (f32[4,512]{1,0:T(4,128)S(1)}, f32[4,168,512]{2,1,0:T(8,128)}, f32[4,168,512]{2,1,0:T(8,128)S(1)}) fusion(f32[4,168,512]{2,1,0:T(8,128)} %get-tuple-element.23, f32[4,512]{1,0:T(4,128)S(1)} %subtract_reduce_fusion.5, f32[4,168,512]{2,1,0:T(8,128)S(1)} %get-tuple-element.42, bf16[4,168,256]{1,2,0:T(8,128)(2,1)S(1)} %all_gather.69, ...), kind=kOutput, calls=%fused_computation.214 | convolution fusion | flops 182695936 | bytes 7520256 | tf_op jit(solution)/shard_map/shr,rc->shc/dot_general | solution.py:67
  77.8 13.3 %all-gather.10 = f32[4,4,512]{2,1,0:T(4,128)S(1)} all-gather(f32[1,4,512]{2,1,0:T(4,128)S(1)} %bitcast.96), channel_id=4, replica_groups=mesh['scen'=2,'hour'=4,'reg'=4] {'hour'}, dimensions={0}, use_global_device_ids=true | all-gather | bytes 40960 | tf_op jit(solution)/shard_map/all_gather | solution.py:69
  96.8 6.4 %reduce-scatter.11.cloned.1.call-done = f32[4,168,64]{1,2,0:T(8,128)} async-done(((f32[4,168,256]{1,2,0:T(8,128)}), f32[4,168,64]{1,2,0:T(8,128)}) %reduce-scatter.11.cloned.1.call-update) | async-done | bytes 172048 | tf_op jit(solution)/shard_map/reduce_scatter | solution.py:81
  104.3 6.6 %all_gather.72 = bf16[4,168,256]{1,2,0:T(8,128)(2,1)S(1)} all-gather(bf16[4,168,64]{1,2,0:T(8,128)(2,1)S(1)} %get-tuple-element.20), channel_id=1, replica_groups=mesh['scen'=2,'hour'=4,'reg'=4] {'reg'}, dimensions={2}, use_global_device_ids=true | all-gather | bytes 430080 | tf_op jit(solution)/shard_map/all_gather | solution.py:84
  110.9 4.0 %fusion.158 = (f32[4,512]{1,0:T(4,128)S(1)}, f32[4,168,512]{2,1,0:T(8,128)}, f32[4,168,512]{2,1,0:T(8,128)S(1)}) fusion(f32[4,168,512]{2,1,0:T(8,128)} %get-tuple-element.19, f32[4,512]{1,0:T(4,128)S(1)} %subtract_reduce_fusion.4, f32[4,168,512]{2,1,0:T(8,128)S(1)} %copy-done.2, bf16[4,168,256]{1,2,0:T(8,128)(2,1)S(1)} %all_gather.72, ...), kind=kOutput, calls=%fused_computation.213 | convolution fusion | flops 182695936 | bytes 7520256 | tf_op jit(solution)/shard_map/shr,rc->shc/dot_general | solution.py:67
  117.6 13.2 %all-gather.11 = f32[4,4,512]{2,1,0:T(4,128)S(1)} all-gather(f32[1,4,512]{2,1,0:T(4,128)S(1)} %bitcast.97), channel_id=5, replica_groups=mesh['scen'=2,'hour'=4,'reg'=4] {'hour'}, dimensions={0}, use_global_device_ids=true | all-gather | bytes 40960 | tf_op jit(solution)/shard_map/all_gather | solution.py:69
  136.4 6.6 %reduce-scatter.13.cloned.1.call-done = f32[4,168,64]{1,2,0:T(8,128)} async-done(((f32[4,168,256]{1,2,0:T(8,128)}), f32[4,168,64]{1,2,0:T(8,128)}) %reduce-scatter.13.cloned.1.call-update) | async-done | bytes 172048 | tf_op jit(solution)/shard_map/reduce_scatter | solution.py:81
  144.0 6.6 %all_gather.75 = bf16[4,168,256]{1,2,0:T(8,128)(2,1)S(1)} all-gather(bf16[4,168,64]{1,2,0:T(8,128)(2,1)S(1)} %fusion.132), channel_id=1, replica_groups=mesh['scen'=2,'hour'=4,'reg'=4] {'reg'}, dimensions={2}, use_global_device_ids=true | all-gather | bytes 430080 | tf_op jit(solution)/shard_map/all_gather | solution.py:84
  150.6 5.4 %fusion.156 = (f32[4,512]{1,0:T(4,128)S(1)}, f32[4,168,512]{2,1,0:T(8,128)}, f32[4,168,512]{2,1,0:T(8,128)S(1)}) fusion(f32[4,168,512]{2,1,0:T(8,128)} %get-tuple-element.17, f32[4,512]{1,0:T(4,128)S(1)} %subtract_reduce_fusion.3, f32[4,168,512]{2,1,0:T(8,128)} %copy-done.3, bf16[4,168,256]{1,2,0:T(8,128)(2,1)S(1)} %all_gather.75, ...), kind=kOutput, calls=%fused_computation.211 | convolution fusion | flops 182695936 | bytes 7520256 | tf_op jit(solution)/shard_map/shr,rc->shc/dot_general | solution.py:67
  157.6 13.2 %all-gather.12 = f32[4,4,512]{2,1,0:T(4,128)S(1)} all-gather(f32[1,4,512]{2,1,0:T(4,128)S(1)} %bitcast.98), channel_id=6, replica_groups=mesh['scen'=2,'hour'=4,'reg'=4] {'hour'}, dimensions={0}, use_global_device_ids=true | all-gather | bytes 40960 | tf_op jit(solution)/shard_map/all_gather | solution.py:69
  175.6 7.4 %reduce-scatter.15.cloned.1.call-done = f32[4,168,64]{1,2,0:T(8,128)} async-done(((f32[4,168,256]{1,2,0:T(8,128)}), f32[4,168,64]{1,2,0:T(8,128)}) %reduce-scatter.15.cloned.1.call-update) | async-done | bytes 172048 | tf_op jit(solution)/shard_map/reduce_scatter | solution.py:81
  184.1 6.8 %all_gather.78 = bf16[4,168,256]{1,2,0:T(8,128)(2,1)S(1)} all-gather(bf16[4,168,64]{1,2,0:T(8,128)(2,1)S(1)} %get-tuple-element.14), channel_id=1, replica_groups=mesh['scen'=2,'hour'=4,'reg'=4] {'reg'}, dimensions={2}, use_global_device_ids=true | all-gather | bytes 430080 | tf_op jit(solution)/shard_map/all_gather | solution.py:84
  190.9 3.6 %fusion.155 = (f32[4,512]{1,0:T(4,128)S(1)}, f32[4,168,512]{2,1,0:T(8,128)}, f32[4,168,512]{2,1,0:T(8,128)S(1)}) fusion(f32[4,168,512]{2,1,0:T(8,128)} %get-tuple-element.13, f32[4,512]{1,0:T(4,128)S(1)} %subtract_reduce_fusion.2, f32[4,168,512]{2,1,0:T(8,128)S(1)} %get-tuple-element.45, bf16[4,168,256]{1,2,0:T(8,128)(2,1)S(1)} %all_gather.78, ...), kind=kOutput, calls=%fused_computation.210 | convolution fusion | flops 182695936 | bytes 7520256 | tf_op jit(solution)/shard_map/shr,rc->shc/dot_general | solution.py:67
  197.2 13.2 %all-gather.13 = f32[4,4,512]{2,1,0:T(4,128)S(1)} all-gather(f32[1,4,512]{2,1,0:T(4,128)S(1)} %bitcast.99), channel_id=7, replica_groups=mesh['scen'=2,'hour'=4,'reg'=4] {'hour'}, dimensions={0}, use_global_device_ids=true | all-gather | bytes 40960 | tf_op jit(solution)/shard_map/all_gather | solution.py:69
  216.1 6.5 %reduce-scatter.17.cloned.1.call-done = f32[4,168,64]{1,2,0:T(8,128)} async-done(((f32[4,168,256]{1,2,0:T(8,128)}), f32[4,168,64]{1,2,0:T(8,128)}) %reduce-scatter.17.cloned.1.call-update) | async-done | bytes 172048 | tf_op jit(solution)/shard_map/reduce_scatter | solution.py:81
  223.6 6.6 %all_gather.81 = bf16[4,168,256]{1,2,0:T(8,128)(2,1)S(1)} all-gather(bf16[4,168,64]{1,2,0:T(8,128)(2,1)S(1)} %fusion.133), channel_id=1, replica_groups=mesh['scen'=2,'hour'=4,'reg'=4] {'reg'}, dimensions={2}, use_global_device_ids=true | all-gather | bytes 430080 | tf_op jit(solution)/shard_map/all_gather | solution.py:84
  230.2 5.4 %fusion.153 = (f32[4,512]{1,0:T(4,128)S(1)}, f32[4,168,512]{2,1,0:T(8,128)}, f32[4,168,512]{2,1,0:T(8,128)S(1)}) fusion(f32[4,168,512]{2,1,0:T(8,128)} %get-tuple-element.11, f32[4,512]{1,0:T(4,128)S(1)} %subtract_reduce_fusion.1, f32[4,168,512]{2,1,0:T(8,128)} %copy-done.5, bf16[4,168,256]{1,2,0:T(8,128)(2,1)S(1)} %all_gather.81, ...), kind=kOutput, calls=%fused_computation.208 | convolution fusion | flops 182695936 | bytes 7520256 | tf_op jit(solution)/shard_map/shr,rc->shc/dot_general | solution.py:67
  237.2 13.2 %all-gather.14 = f32[4,4,512]{2,1,0:T(4,128)S(1)} all-gather(f32[1,4,512]{2,1,0:T(4,128)S(1)} %bitcast.100), channel_id=8, replica_groups=mesh['scen'=2,'hour'=4,'reg'=4] {'hour'}, dimensions={0}, use_global_device_ids=true | all-gather | bytes 40960 | tf_op jit(solution)/shard_map/all_gather | solution.py:69
  250.4 4.0 %collective-permute-start.12 = (f32[4,1,512]{2,1,0:T(1,128)S(1)}, f32[4,1,512]{2,1,0:T(1,128)}, u32[]{:S(2)}, u32[]{:S(2)}) collective-permute-start(f32[4,1,512]{2,1,0:T(1,128)S(1)} %get-tuple-element.28), channel_id=1, source_target_pairs={{0,4},{4,8},{8,12},{1,5},{5,9},{9,13},{2,6},{6,10},{10,14},{3,7},{... | collective-permute-start | bytes 24584 | tf_op jit(solution)/shard_map/ppermute | solution.py:23
  255.8 6.8 %reduce-scatter.19.cloned.1.call-done = f32[4,168,64]{1,2,0:T(8,128)} async-done(((f32[4,168,256]{1,2,0:T(8,128)}), f32[4,168,64]{1,2,0:T(8,128)}) %reduce-scatter.19.cloned.1.call-update) | async-done | bytes 172048 | tf_op jit(solution)/shard_map/reduce_scatter | solution.py:81
  263.7 6.6 %all_gather.84 = bf16[4,168,256]{1,2,0:T(8,128)(2,1)S(1)} all-gather(bf16[4,168,64]{1,2,0:T(8,128)(2,1)S(1)} %get-tuple-element.8), channel_id=1, replica_groups=mesh['scen'=2,'hour'=4,'reg'=4] {'reg'}, dimensions={2}, use_global_device_ids=true | all-gather | bytes 430080 | tf_op jit(solution)/shard_map/all_gather | solution.py:84
  281.1 19.9 %reduce-scatter.21.cloned.1.call-done = f32[4,168,64]{1,2,0:T(8,128)} async-done(((f32[4,168,256]{1,2,0:T(8,128)}), f32[4,168,64]{1,2,0:T(8,128)}) %reduce-scatter.21.cloned.1.call-update) | async-done | bytes 172048 | tf_op jit(solution)/shard_map/reduce_scatter | solution.py:81
  302.1 6.6 %all_gather.87 = bf16[4,168,256]{1,2,0:T(8,128)(2,1)S(1)} all-gather(bf16[4,168,64]{1,2,0:T(8,128)(2,1)S(1)} %fusion.134), channel_id=1, replica_groups=mesh['scen'=2,'hour'=4,'reg'=4] {'reg'}, dimensions={2}, use_global_device_ids=true | all-gather | bytes 430080 | tf_op jit(solution)/shard_map/all_gather | solution.py:84
  314.4 13.2 %all-gather.15 = f32[4,4,512]{2,1,0:T(4,128)S(1)} all-gather(f32[1,4,512]{2,1,0:T(4,128)S(1)} %bitcast.94), channel_id=9, replica_groups=mesh['scen'=2,'hour'=4,'reg'=4] {'hour'}, dimensions={0}, use_global_device_ids=true | all-gather | bytes 40960 | tf_op jit(solution)/shard_map/all_gather | solution.py:69
  328.0 8.3 %all-reduce = (f32[3,4,512]{2,1,0:T(4,128)S(1)}, f32[3,4]{1,0:T(4,128)S(1)}) all-reduce(f32[3,4,512]{2,1,0:T(4,128)S(1)} %fusion.135, f32[3,4]{1,0:T(4,128)S(1)} %bitcast.101), channel_id=1, replica_groups=mesh['scen'=2,'hour'=4,'reg'=4] {'scen'}, use_global_device_ids=true, to_apply=%region_31.0 | all-reduce | flops 6156 | bytes 49248 | tf_op jit(solution)/shard_map/psum | solution.py:96
  (163 shorter events, 72.4 us)
Async XLA Ops:
  7.2 30.7 %copy-start = (f32[4,168,256]{2,1,0:T(8,128)S(1)}, f32[4,168,256]{2,1,0:T(8,128)}, u32[]{:S(2)}) copy-start(f32[4,168,256]{2,1,0:T(8,128)} %param.17) | copy-start | bytes 2064388
  7.2 23.4 %copy-start.22 = (f32[3,512]{1,0:T(4,128)S(1)}, f32[3,512]{1,0:T(4,128)}, u32[]{:S(2)}) copy-start(f32[3,512]{1,0:T(4,128)} %param.14) | copy-start | bytes 18436
  7.2 23.4 %copy-start.19 = (f32[4,168,256]{2,1,0:T(8,128)S(1)}, f32[4,168,256]{2,1,0:T(8,128)}, u32[]{:S(2)}) copy-start(f32[4,168,256]{2,1,0:T(8,128)} %param.19) | copy-start | bytes 2064388
  7.3 56.6 %reduce-scatter.9.cloned.1.call-start = ((), (), s32[]{:S(2)}) async-start(), calls=%async_computation.8 | async-start | bytes 1310720 | tf_op jit(solution)/shard_map/reduce_scatter | solution.py:81
  8.3 22.4 %collective-permute-start = (f32[4,1,512]{2,1,0:T(1,128)S(1)}, f32[4,1,512]{2,1,0:T(1,128)S(1)}, u32[]{:S(2)}, u32[]{:S(2)}) collective-permute-start(f32[4,1,512]{2,1,0:T(1,128)S(1)} %get-tuple-element.40), channel_id=1, source_target_pairs={{0,4},{4,8},{8,12},{1,5},{5,9},{9,13},{2,6},{6,10},{10,14},{3,7},{... | collective-permute-start | bytes 24584 | tf_op jit(solution)/shard_map/ppermute | solution.py:23
  13.3 17.4 %collective-permute-start.1 = (f32[4,1,512]{2,1,0:T(1,128)S(1)}, f32[4,1,512]{2,1,0:T(1,128)S(1)}, u32[]{:S(2)}, u32[]{:S(2)}) collective-permute-start(f32[4,1,512]{2,1,0:T(1,128)S(1)} %get-tuple-element.41), channel_id=1, source_target_pairs={{4,0},{8,4},{12,8},{5,1},{9,5},{13,9},{6,2},{10,6},{14,10},{7,3},{... | collective-permute-start | bytes 24584 | tf_op jit(solution)/shard_map/ppermute | solution.py:25
  37.9 65.4 %reduce-scatter.11.cloned.1.call-start = ((), (), s32[]{:S(2)}) async-start(), calls=%async_computation.9 | async-start | bytes 1310720 | tf_op jit(solution)/shard_map/reduce_scatter | solution.py:81
  52.8 18.8 %collective-permute-start.2 = (f32[4,1,512]{2,1,0:T(1,128)S(1)}, f32[4,1,512]{2,1,0:T(1,128)S(1)}, u32[]{:S(2)}, u32[]{:S(2)}) collective-permute-start(f32[4,1,512]{2,1,0:T(1,128)S(1)} %get-tuple-element.38), channel_id=1, source_target_pairs={{0,4},{4,8},{8,12},{1,5},{5,9},{9,13},{2,6},{6,10},{10,14},{3,7},{... | collective-permute-start | bytes 24584 | tf_op jit(solution)/shard_map/ppermute | solution.py:23
  56.3 15.3 %collective-permute-start.3 = (f32[4,1,512]{2,1,0:T(1,128)S(1)}, f32[4,1,512]{2,1,0:T(1,128)S(1)}, u32[]{:S(2)}, u32[]{:S(2)}) collective-permute-start(f32[4,1,512]{2,1,0:T(1,128)S(1)} %get-tuple-element.39), channel_id=1, source_target_pairs={{4,0},{8,4},{12,8},{5,1},{9,5},{13,9},{6,2},{10,6},{14,10},{7,3},{... | collective-permute-start | bytes 24584 | tf_op jit(solution)/shard_map/ppermute | solution.py:25
  77.7 25.5 %copy-start.14 = (f32[4,168,64]{1,2,0:T(8,128)S(1)}, f32[4,168,64]{1,2,0:T(8,128)}, u32[]{:S(2)}) copy-start(f32[4,168,64]{1,2,0:T(8,128)} %reduce-scatter.9.cloned.1.call-done) | copy-start | bytes 516100
  77.8 33.2 %copy-start.2 = (f32[4,168,512]{2,1,0:T(8,128)S(1)}, f32[4,168,512]{2,1,0:T(8,128)}, u32[]{:S(2)}) copy-start(f32[4,168,512]{2,1,0:T(8,128)} %copy-done.1) | copy-start | bytes 4128772
  77.8 65.2 %reduce-scatter.13.cloned.1.call-start = ((), (), s32[]{:S(2)}) async-start(), calls=%async_computation.10 | async-start | bytes 1310720 | tf_op jit(solution)/shard_map/reduce_scatter | solution.py:81
  92.0 18.9 %collective-permute-start.4 = (f32[4,1,512]{2,1,0:T(1,128)S(1)}, f32[4,1,512]{2,1,0:T(1,128)S(1)}, u32[]{:S(2)}, u32[]{:S(2)}) collective-permute-start(f32[4,1,512]{2,1,0:T(1,128)S(1)} %get-tuple-element.36), channel_id=1, source_target_pairs={{0,4},{4,8},{8,12},{1,5},{5,9},{9,13},{2,6},{6,10},{10,14},{3,7},{... | collective-permute-start | bytes 24584 | tf_op jit(solution)/shard_map/ppermute | solution.py:23
  95.5 15.5 %collective-permute-start.5 = (f32[4,1,512]{2,1,0:T(1,128)S(1)}, f32[4,1,512]{2,1,0:T(1,128)S(1)}, u32[]{:S(2)}, u32[]{:S(2)}) collective-permute-start(f32[4,1,512]{2,1,0:T(1,128)S(1)} %get-tuple-element.37), channel_id=1, source_target_pairs={{4,0},{8,4},{12,8},{5,1},{9,5},{13,9},{6,2},{10,6},{14,10},{7,3},{... | collective-permute-start | bytes 24584 | tf_op jit(solution)/shard_map/ppermute | solution.py:25
  117.5 65.5 %reduce-scatter.15.cloned.1.call-start = ((), (), s32[]{:S(2)}) async-start(), calls=%async_computation.11 | async-start | bytes 1310720 | tf_op jit(solution)/shard_map/reduce_scatter | solution.py:81
  131.7 19.0 %collective-permute-start.6 = (f32[4,1,512]{2,1,0:T(1,128)S(1)}, f32[4,1,512]{2,1,0:T(1,128)S(1)}, u32[]{:S(2)}, u32[]{:S(2)}) collective-permute-start(f32[4,1,512]{2,1,0:T(1,128)S(1)} %get-tuple-element.34), channel_id=1, source_target_pairs={{0,4},{4,8},{8,12},{1,5},{5,9},{9,13},{2,6},{6,10},{10,14},{3,7},{... | collective-permute-start | bytes 24584 | tf_op jit(solution)/shard_map/ppermute | solution.py:23
  135.1 15.6 %collective-permute-start.7 = (f32[4,1,512]{2,1,0:T(1,128)S(1)}, f32[4,1,512]{2,1,0:T(1,128)S(1)}, u32[]{:S(2)}, u32[]{:S(2)}) collective-permute-start(f32[4,1,512]{2,1,0:T(1,128)S(1)} %get-tuple-element.35), channel_id=1, source_target_pairs={{4,0},{8,4},{12,8},{5,1},{9,5},{13,9},{6,2},{10,6},{14,10},{7,3},{... | collective-permute-start | bytes 24584 | tf_op jit(solution)/shard_map/ppermute | solution.py:25
  157.5 25.5 %copy-start.15 = (f32[4,168,64]{1,2,0:T(8,128)S(1)}, f32[4,168,64]{1,2,0:T(8,128)}, u32[]{:S(2)}) copy-start(f32[4,168,64]{1,2,0:T(8,128)} %reduce-scatter.13.cloned.1.call-done) | copy-start | bytes 516100
  157.5 65.1 %reduce-scatter.17.cloned.1.call-start = ((), (), s32[]{:S(2)}) async-start(), calls=%async_computation.12 | async-start | bytes 1310720 | tf_op jit(solution)/shard_map/reduce_scatter | solution.py:81
  170.8 20.1 %collective-permute-start.8 = (f32[4,1,512]{2,1,0:T(1,128)S(1)}, f32[4,1,512]{2,1,0:T(1,128)S(1)}, u32[]{:S(2)}, u32[]{:S(2)}) collective-permute-start(f32[4,1,512]{2,1,0:T(1,128)S(1)} %get-tuple-element.32), channel_id=1, source_target_pairs={{0,4},{4,8},{8,12},{1,5},{5,9},{9,13},{2,6},{6,10},{10,14},{3,7},{... | collective-permute-start | bytes 24584 | tf_op jit(solution)/shard_map/ppermute | solution.py:23
  174.2 16.7 %collective-permute-start.9 = (f32[4,1,512]{2,1,0:T(1,128)S(1)}, f32[4,1,512]{2,1,0:T(1,128)S(1)}, u32[]{:S(2)}, u32[]{:S(2)}) collective-permute-start(f32[4,1,512]{2,1,0:T(1,128)S(1)} %get-tuple-element.33), channel_id=1, source_target_pairs={{4,0},{8,4},{12,8},{5,1},{9,5},{13,9},{6,2},{10,6},{14,10},{7,3},{... | collective-permute-start | bytes 24584 | tf_op jit(solution)/shard_map/ppermute | solution.py:25
  197.1 65.5 %reduce-scatter.19.cloned.1.call-start = ((), (), s32[]{:S(2)}) async-start(), calls=%async_computation.13 | async-start | bytes 1310720 | tf_op jit(solution)/shard_map/reduce_scatter | solution.py:81
  211.2 19.0 %collective-permute-start.10 = (f32[4,1,512]{2,1,0:T(1,128)S(1)}, f32[4,1,512]{2,1,0:T(1,128)S(1)}, u32[]{:S(2)}, u32[]{:S(2)}) collective-permute-start(f32[4,1,512]{2,1,0:T(1,128)S(1)} %get-tuple-element.30), channel_id=1, source_target_pairs={{0,4},{4,8},{8,12},{1,5},{5,9},{9,13},{2,6},{6,10},{10,14},{3,7},{... | collective-permute-start | bytes 24584 | tf_op jit(solution)/shard_map/ppermute | solution.py:23
  214.7 15.6 %collective-permute-start.11 = (f32[4,1,512]{2,1,0:T(1,128)S(1)}, f32[4,1,512]{2,1,0:T(1,128)S(1)}, u32[]{:S(2)}, u32[]{:S(2)}) collective-permute-start(f32[4,1,512]{2,1,0:T(1,128)S(1)} %get-tuple-element.31), channel_id=1, source_target_pairs={{4,0},{8,4},{12,8},{5,1},{9,5},{13,9},{6,2},{10,6},{14,10},{7,3},{... | collective-permute-start | bytes 24584 | tf_op jit(solution)/shard_map/ppermute | solution.py:25
  237.1 25.5 %copy-start.16 = (f32[4,168,64]{1,2,0:T(8,128)S(1)}, f32[4,168,64]{1,2,0:T(8,128)}, u32[]{:S(2)}) copy-start(f32[4,168,64]{1,2,0:T(8,128)} %reduce-scatter.17.cloned.1.call-done) | copy-start | bytes 516100
  237.1 63.9 %reduce-scatter.21.cloned.1.call-start = ((), (), s32[]{:S(2)}) async-start(), calls=%async_computation.14 | async-start | bytes 1310720 | tf_op jit(solution)/shard_map/reduce_scatter | solution.py:81
  250.4 20.0 %collective-permute-start.12 = (f32[4,1,512]{2,1,0:T(1,128)S(1)}, f32[4,1,512]{2,1,0:T(1,128)}, u32[]{:S(2)}, u32[]{:S(2)}) collective-permute-start(f32[4,1,512]{2,1,0:T(1,128)S(1)} %get-tuple-element.28), channel_id=1, source_target_pairs={{0,4},{4,8},{8,12},{1,5},{5,9},{9,13},{2,6},{6,10},{10,14},{3,7},{... | collective-permute-start | bytes 24584 | tf_op jit(solution)/shard_map/ppermute | solution.py:23
  254.4 16.0 %collective-permute-start.13 = (f32[4,1,512]{2,1,0:T(1,128)S(1)}, f32[4,1,512]{2,1,0:T(1,128)}, u32[]{:S(2)}, u32[]{:S(2)}) collective-permute-start(f32[4,1,512]{2,1,0:T(1,128)S(1)} %get-tuple-element.29), channel_id=1, source_target_pairs={{4,0},{8,4},{12,8},{5,1},{9,5},{13,9},{6,2},{10,6},{14,10},{7,3},{... | collective-permute-start | bytes 24584 | tf_op jit(solution)/shard_map/ppermute | solution.py:25
  275.5 64.2 %reduce-scatter.23.cloned.1.call-start = ((), (), s32[]{:S(2)}) async-start(), calls=%async_computation.15 | async-start | bytes 1310720 | tf_op jit(solution)/shard_map/reduce_scatter | solution.py:81
  276.4 32.3 %collective-permute-start.14 = (f32[4,1,512]{2,1,0:T(1,128)S(1)}, f32[4,1,512]{2,1,0:T(1,128)S(1)}, u32[]{:S(2)}, u32[]{:S(2)}) collective-permute-start(f32[4,1,512]{2,1,0:T(1,128)S(1)} %get-tuple-element.26), channel_id=1, source_target_pairs={{0,4},{4,8},{8,12},{1,5},{5,9},{9,13},{2,6},{6,10},{10,14},{3,7},{... | collective-permute-start | bytes 24584 | tf_op jit(solution)/shard_map/ppermute | solution.py:23
  279.8 28.9 %collective-permute-start.15 = (f32[4,1,512]{2,1,0:T(1,128)S(1)}, f32[4,1,512]{2,1,0:T(1,128)S(1)}, u32[]{:S(2)}, u32[]{:S(2)}) collective-permute-start(f32[4,1,512]{2,1,0:T(1,128)S(1)} %get-tuple-element.27), channel_id=1, source_target_pairs={{4,0},{8,4},{12,8},{5,1},{9,5},{13,9},{6,2},{10,6},{14,10},{7,3},{... | collective-permute-start | bytes 24584 | tf_op jit(solution)/shard_map/ppermute | solution.py:25
  314.2 25.6 %copy-start.13 = (f32[4,168,64]{1,2,0:T(8,128)S(1)}, f32[4,168,64]{1,2,0:T(8,128)}, u32[]{:S(2)}) copy-start(f32[4,168,64]{1,2,0:T(8,128)} %reduce-scatter.21.cloned.1.call-done) | copy-start | bytes 516100
  (20 other events, 186.6 us)
Sparse Core Ops, SparseCore 0:
  38.0 25.8 reduce-scatter.8
  77.9 25.3 reduce-scatter.10
  117.6 25.3 reduce-scatter.12
  157.6 25.3 reduce-scatter.14
  197.2 25.3 reduce-scatter.16
  237.2 25.3 reduce-scatter.18
  275.6 25.3 reduce-scatter.20
  314.3 25.3 reduce-scatter.22
